TPU v7x, 512 devices: a whole 4x4x16 slice. The times are simulated.
512 devices in a mesh: col: 64 (over y, z), row: 8 (over x, core).
Axes of the slice: x: 4, y: 4, z: 16, core: 2. Of those that a mesh axis runs over, the one named last changes fastest.
Arguments:
- x_block: bfloat16 [8, 8192, 64], P('row', 'col'), may hold values from -6 to 6
- tiles: bfloat16 [64, 8, 96, 128, 128], P('col', 'row'), may hold values from -0.078125 to 0.078125
- tile_rows: int32 [64, 8, 96], P('col', 'row'), may hold values from 0 to 63
- tile_cols: int32 [64, 8, 96], P('col', 'row'), may hold values from 0 to 7
- tile_count: int32 [64, 8], P('col', 'row'), may hold values from 1 to 96, as said below
Outputs:
- filtered: bfloat16 [8, 8192, 64], P('row', 'col')
- gram: float32 [64, 64], replicated
Inputs may be any that keep to these rules, and one draw needn't show every extreme that they name: `tile_count`: padding slots hold arbitrary tiles and indices; every draw has some device with all 96 slots live.
All inputs are finite; a program needn't handle non-finite values.
Results may differ from a plain program's by a relative error of at most 0.0049.
Values may be sent and summed in bfloat16 or wider, within the bound.
A program may use at most 64 MiB of HBM per device.

v0:
```python
import jax
import jax.numpy as jnp
from jax import lax
from jax.sharding import PartitionSpec as P


def local(x_block, tiles, tile_rows, tile_cols, tile_count):
    n_col = lax.axis_size("col")
    n_row = lax.axis_size("row")
    tile_data = tiles[0, 0]
    rows_here = tile_rows[0, 0]
    cols_here = tile_cols[0, 0]
    count_here = tile_count[0, 0]
    vectors = x_block.shape[2]
    slots = tile_data.shape[0]
    live = jnp.arange(slots, dtype=jnp.int32) < count_here
    placing = (
        (rows_here[None, :] == jnp.arange(n_col, dtype=jnp.int32)[:, None]) & live[None, :]
    ).astype(jnp.float32)

    def apply_local(segment):
        slab_vecs = lax.all_gather(segment[0], "row", axis=0, tiled=True)
        picked = slab_vecs.reshape(n_row, 128, vectors)[cols_here]
        products = jnp.einsum("tij,tjk->tik", tile_data, picked, preferred_element_type=jnp.float32)
        products = products.reshape(slots, 128 * vectors)
        band_sums = jnp.dot(placing, products, precision=lax.Precision.HIGH)
        owned = lax.psum_scatter(band_sums, "col", scatter_dimension=0, tiled=True)
        return owned.reshape(1, 128, vectors)

    first = apply_local(x_block).astype(jnp.bfloat16)
    second = apply_local(first)
    gram_term = jnp.dot(first[0].astype(jnp.float32).T, second[0], precision=lax.Precision.HIGHEST)
    gram = lax.psum(gram_term, ("col", "row")) / (n_col * n_row * 128)
    return (second.astype(jnp.bfloat16), gram)


def solution(mesh):
    placed = (
        P("row", "col", None),
        P("col", "row", None, None, None),
        P("col", "row", None),
        P("col", "row", None),
        P("col", "row"),
    )
    return jax.shard_map(
        local, mesh=mesh, in_specs=placed, out_specs=(P("row", "col", None), P()), check_vma=False
    )
```

profile of v0, /device:TPU:1, one launch (start us, length us, event | category | flops | bytes accessed | tf_op | source)
XLA Modules:
  0.0 760.7 jit_solution(15123610081769181831)
XLA Ops:
  7.2 0.0 copy-start
  7.2 0.0 all-reduce.5.cloned.1.call-start
  8.0 0.7 fusion.20
  8.8 18.2 %all-gather = bf16[1,1024,64]{1,2,0:T(8,128)(2,1)S(1)} all-gather(bf16[1,128,64]{1,2,0:T(8,128)(2,1)} %param.5), channel_id=2, replica_groups=mesh['col'=64,'row'=8] {'row'}, dimensions={1}, use_global_device_ids=true | all-gather | bytes 147456 | tf_op jit(solution)/shard_map/all_gather | solution.py:22
  27.1 2.0 gather_fusion
  29.0 0.0 copy-done
  29.0 5.3 fusion.4
  34.4 0.0 copy-start.3
  34.4 5.1 copy.18
  39.4 0.0 copy-done.3
  39.4 5.1 fusion.14
  44.5 250.4 %all-reduce.6 = bf16[64,8192]{1,0:T(8,128)(2,1)} all-reduce(f32[64,8192]{1,0:T(8,128)} %fusion.14), channel_id=3, replica_groups=mesh['col'=64,'row'=8] {'col'}, use_global_device_ids=true, to_apply=%region_0.0.clone | all-reduce | flops 524288 | bytes 3145728
  294.9 1.3 dynamic-slice
  296.2 1.7 fusion.10
  297.9 0.1 convert_element_type.27
  298.0 0.0 copy-start.1
  298.0 66.5 %all_gather.7 = bf16[1024,64]{1,0:T(8,128)(2,1)S(1)} all-gather(bf16[128,64]{1,0:T(8,128)(2,1)S(1)} %convert_element_type.27), channel_id=1, replica_groups=mesh['col'=64,'row'=8] {'row'}, dimensions={0}, use_global_device_ids=true | all-gather | bytes 147456 | tf_op jit(solution)/shard_map/all_gather | solution.py:22
  364.5 0.0 copy-done.1
  364.5 0.1 copy.20
  364.6 2.0 gather_fusion.1
  366.6 5.3 fusion.7
  371.9 5.1 copy.21
  377.0 0.0 copy-start.2
  377.0 5.1 fusion.12
  382.0 0.0 all-reduce.5.cloned.1.call-update
  382.1 257.0 %all-reduce.5.cloned.1.call-done = f32[64,8192]{1,0:T(8,128)} async-done(((f32[64,8192]{1,0:T(8,128)}), f32[64,8192]{1,0:T(8,128)}) %all-reduce.5.cloned.1.call-update) | async-done | bytes 2097168
  639.1 1.7 convert_reduce_fusion
  640.8 0.1 convert_element_type.29
  640.9 0.7 copy.22
  641.6 1.7 dynamic-slice_reduce_fusion
  643.3 0.1 squeeze_reshape.3
  643.4 0.0 copy-done.2
  643.4 0.2 fusion.21
  643.6 109.7 %psum.7 = f32[64,64]{1,0:T(8,128)S(1)} all-reduce(f32[64,64]{1,0:T(8,128)S(1)} %fusion.21), channel_id=1, replica_groups=mesh['col'=64,'row'=8] {'col','row'}, use_global_device_ids=true, to_apply=%region_2.0 | all-reduce | flops 4096 | bytes 32768 | tf_op jit(solution)/shard_map/psum | solution.py:33
  753.3 0.6 broadcast_multiply_fusion
  (4 shorter events, 0.1 us)
Async XLA Ops:
  7.2 21.8 %copy-start = (bf16[1,1,96,128,128]{4,3,2,1,0:T(8,128)(2,1)S(1)}, bf16[1,1,96,128,128]{4,3,2,1,0:T(8,128)(2,1)}, u32[]{:S(2)}) copy-start(bf16[1,1,96,128,128]{4,3,2,1,0:T(8,128)(2,1)} %param.6) | copy-start | bytes 9437188
  7.2 631.9 %all-reduce.5.cloned.1.call-start = ((), (), s32[]{:S(2)}) async-start(), calls=%async_computation | async-start | bytes 4194304
  34.4 5.1 copy-start.3
  298.0 66.5 %copy-start.1 = (bf16[128,64]{1,0:T(8,128)(2,1)}, bf16[128,64]{1,0:T(8,128)(2,1)S(1)}, u32[]{:S(2)}) copy-start(bf16[128,64]{1,0:T(8,128)(2,1)S(1)} %convert_element_type.27) | copy-start | bytes 49156
  377.0 266.4 %copy-start.2 = (bf16[128,64]{1,0:T(8,128)(2,1)S(1)}, bf16[128,64]{1,0:T(8,128)(2,1)}, u32[]{:S(2)}) copy-start(bf16[128,64]{1,0:T(8,128)(2,1)} %copy-done.1) | copy-start | bytes 49156
Sparse Core Ops, SparseCore 0:
  382.2 256.8 all-reduce.4
where the time goes:
time: 761 us
  blocking collectives  445 us (58%)
  waiting for transfers between devices  257 us (34%)
  local copies, waits for them, and re-layouts  21.7 us (3%)
  matrix products  21 us (3%)
  between operations  14.9 us (2%)
    unnamed x2, waiting for transfers between devices  257 us
    unnamed x1, blocking collectives  250 us
    psum x1, blocking collectives, local(): gram = lax.psum(gram_term, ('col', 'row')) / (n_col * n_row * 128)  110 us
    all_gather x2, blocking collectives, apply_local(): slab_vecs = lax.all_gather(segment[0], 'row', axis=0, tiled=True)  84.7 us
  transfers between devices with their start and end apart: 1, of which 1 were waited for; matrix products, arithmetic and copies ran while one was open for 0% of the time, Pallas kernels for 0%

commit v1 on v0

--- a/solution.py
+++ b/solution.py
@@ -30,7 +30,7 @@
     first = apply_local(x_block).astype(jnp.bfloat16)
     second = apply_local(first)
     gram_term = jnp.dot(first[0].astype(jnp.float32).T, second[0], precision=lax.Precision.HIGHEST)
-    gram = lax.psum(gram_term, ("col", "row")) / (n_col * n_row * 128)
+    gram = jnp.sum(lax.all_gather(gram_term, ("col", "row")), axis=0) / (n_col * n_row * 128)
     return (second.astype(jnp.bfloat16), gram)
 
 

time: 761 us -> 885 us (1.16)
  waiting for transfers between devices: 257 us -> 483 us
  blocking collectives: 445 us -> 335 us
    all_gather x0 -> x1, waiting for transfers between devices: none -> 225 us  [local(): lax.all_gather(gram_term, ('col', 'row'))]
    psum x1 -> x0, blocking collectives: 110 us -> none  [local(): gram = lax.psum(gram_term, ('col', 'row')) / (n_col * n_row * 128)]
    unnamed x2 -> x3, waiting for transfers between devices: 257 us -> 258 us
  transfers between devices with their start and end apart: 1 -> 2, of which waited for: 1 -> 2; matrix products, arithmetic and copies ran while one was open for 0% -> 0% of each run, Pallas kernels for 0% -> 0%
where the time goes in v1:
time: 885 us; the launch traced here: 884 us
  waiting for transfers between devices  483 us (55%)
  blocking collectives  335 us (38%)
  matrix products  21.7 us (2%)
  local copies, waits for them, and re-layouts  21.5 us (2%)
  between operations  14.9 us (2%)
    unnamed x3, waiting for transfers between devices  258 us
    unnamed x1, blocking collectives  250 us
    all_gather x1, waiting for transfers between devices, local(): lax.all_gather(gram_term, ('col', 'row'))  225 us
    all_gather x2, blocking collectives, apply_local(): slab_vecs = lax.all_gather(segment[0], 'row', axis=0, tiled=True)  84.7 us
  transfers between devices with their start and end apart: 2, of which 2 were waited for; matrix products, arithmetic and copies ran while one was open for 0% of the time, Pallas kernels for 0%

profile of v1, /device:TPU:1, one launch (start us, length us, event | category | flops | bytes accessed | tf_op | source)
XLA Modules:
  0.0 884.2 jit_solution(2235849170609126572)
XLA Ops:
  7.2 0.0 copy-start
  7.2 0.0 all-reduce.5.cloned.1.call-start
  8.0 0.7 fusion.20
  8.8 18.2 %all-gather = bf16[1,1024,64]{1,2,0:T(8,128)(2,1)S(1)} all-gather(bf16[1,128,64]{1,2,0:T(8,128)(2,1)} %param.5), channel_id=2, replica_groups=mesh['col'=64,'row'=8] {'row'}, dimensions={1}, use_global_device_ids=true | all-gather | bytes 147456 | tf_op jit(solution)/shard_map/all_gather | solution.py:22
  27.1 2.0 gather_fusion
  29.0 0.0 copy-done
  29.0 5.3 fusion.4
  34.4 0.0 copy-start.3
  34.4 5.1 copy.18
  39.4 0.0 copy-done.3
  39.4 5.1 fusion.14
  44.5 250.4 %all-reduce.6 = bf16[64,8192]{1,0:T(8,128)(2,1)} all-reduce(f32[64,8192]{1,0:T(8,128)} %fusion.14), channel_id=4, replica_groups=mesh['col'=64,'row'=8] {'col'}, use_global_device_ids=true, to_apply=%region_0.0.clone | all-reduce | flops 524288 | bytes 3145728
  294.9 1.3 dynamic-slice
  296.1 1.7 fusion.10
  297.8 0.1 convert_element_type.27
  297.9 0.0 copy-start.1
  297.9 66.5 %all_gather.13 = bf16[1024,64]{1,0:T(8,128)(2,1)S(1)} all-gather(bf16[128,64]{1,0:T(8,128)(2,1)S(1)} %convert_element_type.27), channel_id=1, replica_groups=mesh['col'=64,'row'=8] {'row'}, dimensions={0}, use_global_device_ids=true | all-gather | bytes 147456 | tf_op jit(solution)/shard_map/all_gather | solution.py:22
  364.3 0.0 copy-done.1
  364.4 0.1 copy.20
  364.5 2.0 gather_fusion.1
  366.4 5.3 fusion.7
  371.8 5.1 copy.21
  376.8 0.0 copy-start.2
  376.8 5.1 fusion.12
  381.9 0.0 all-reduce.5.cloned.1.call-update
  382.0 0.0 all-gather.4.cloned.1.call-start
  382.0 257.5 %all-reduce.5.cloned.1.call-done = f32[64,8192]{1,0:T(8,128)} async-done(((f32[64,8192]{1,0:T(8,128)}), f32[64,8192]{1,0:T(8,128)}) %all-reduce.5.cloned.1.call-update) | async-done | bytes 2097168
  639.6 1.7 dynamic-slice_reduce_fusion
  641.2 0.1 squeeze_reshape.3
  641.3 0.0 copy-done.2
  641.3 0.8 fusion.21
  642.1 0.0 all-gather.4.cloned.1.call-update
  642.2 1.7 convert_reduce_fusion
  643.9 0.1 convert_element_type.29
  644.0 0.7 copy.22
  644.7 225.1 %all-gather.4.cloned.1.call-done = f32[32768,64]{1,0:T(8,128)} async-done(((f32[64,64]{1,0:T(8,128)}), f32[32768,64]{1,0:T(8,128)}) %all-gather.4.cloned.1.call-update) | async-done | bytes 8388624 | tf_op jit(solution)/shard_map/all_gather | solution.py:33
  869.8 6.9 reduce_sum.9
  876.7 0.6 broadcast_multiply_fusion
  (4 shorter events, 0.1 us)
Async XLA Ops:
  7.2 21.8 %copy-start = (bf16[1,1,96,128,128]{4,3,2,1,0:T(8,128)(2,1)S(1)}, bf16[1,1,96,128,128]{4,3,2,1,0:T(8,128)(2,1)}, u32[]{:S(2)}) copy-start(bf16[1,1,96,128,128]{4,3,2,1,0:T(8,128)(2,1)} %param.6) | copy-start | bytes 9437188
  7.2 632.4 %all-reduce.5.cloned.1.call-start = ((), (), s32[]{:S(2)}) async-start(), calls=%async_computation.1 | async-start | bytes 4194304
  34.4 5.1 copy-start.3
  297.9 66.5 %copy-start.1 = (bf16[128,64]{1,0:T(8,128)(2,1)}, bf16[128,64]{1,0:T(8,128)(2,1)S(1)}, u32[]{:S(2)}) copy-start(bf16[128,64]{1,0:T(8,128)(2,1)S(1)} %convert_element_type.27) | copy-start | bytes 49156
  376.8 264.5 %copy-start.2 = (bf16[128,64]{1,0:T(8,128)(2,1)S(1)}, bf16[128,64]{1,0:T(8,128)(2,1)}, u32[]{:S(2)}) copy-start(bf16[128,64]{1,0:T(8,128)(2,1)} %copy-done.1) | copy-start | bytes 49156
  382.0 487.8 %all-gather.4.cloned.1.call-start = ((), (), s32[]{:S(2)}) async-start(), calls=%async_computation | async-start | bytes 16809984 | tf_op jit(solution)/shard_map/all_gather | solution.py:33
Sparse Core Ops, SparseCore 0:
  382.1 257.4 all-reduce.4
  645.5 224.1 all-gather.3

commit v2 on v0

--- a/solution.py
+++ b/solution.py
@@ -19,7 +19,14 @@
     ).astype(jnp.float32)
 
     def apply_local(segment):
-        slab_vecs = lax.all_gather(segment[0], "row", axis=0, tiled=True)
+        ring = [segment[0]]
+        for hop in range(7):
+            ring.append(lax.ppermute(ring[-1], "row", [(dev, (dev + 1) % 8) for dev in range(8)]))
+        slab_vecs = jnp.roll(
+            jnp.concatenate(ring[::-1], axis=0),
+            (lax.axis_index("row") + 1) * ring[0].shape[0],
+            axis=0,
+        )
         picked = slab_vecs.reshape(n_row, 128, vectors)[cols_here]
         products = jnp.einsum("tij,tjk->tik", tile_data, picked, preferred_element_type=jnp.float32)
         products = products.reshape(slots, 128 * vectors)

time: 761 us -> 796 us (1.046)
  blocking collectives: 445 us -> 359 us
  waiting for transfers between devices: 257 us -> 320 us
  starting transfers between devices: 0.04 us -> 56.3 us
    all_gather x2 -> x0, blocking collectives: 84.7 us -> none  [apply_local(): slab_vecs = lax.all_gather(segment[0], 'row', axis=0, tiled=True)]
    ppermute x0 -> x14, waiting for transfers between devices: none -> 60.7 us  [apply_local(): lax.ppermute(ring[-1], 'row', [(dev, (dev + 1) % 8) for dev in range(8)])]
    ppermute x0 -> x14, starting transfers between devices: none -> 56.2 us  [apply_local(): lax.ppermute(ring[-1], 'row', [(dev, (dev + 1) % 8) for dev in range(8)])]
  transfers between devices with their start and end apart: 1 -> 15, of which waited for: 1 -> 15; matrix products, arithmetic and copies ran while one was open for 0% -> 0% of each run, Pallas kernels for 0% -> 0%
where the time goes in v2:
time: 796 us
  blocking collectives  359 us (45%)
  waiting for transfers between devices  320 us (40%)
  starting transfers between devices  56.3 us (7%)
  local copies, waits for them, and re-layouts  22.4 us (3%)
  matrix products  21 us (3%)
  between operations  14.8 us (2%)
    unnamed x2, waiting for transfers between devices  260 us
    unnamed x1, blocking collectives  249 us
    psum x1, blocking collectives, local(): gram = lax.psum(gram_term, ('col', 'row')) / (n_col * n_row * 128)  110 us
    ppermute x14, waiting for transfers between devices, apply_local(): lax.ppermute(ring[-1], 'row', [(dev, (dev + 1) % 8) for dev in range(8)])  60.7 us
    ppermute x14, starting transfers between devices, apply_local(): lax.ppermute(ring[-1], 'row', [(dev, (dev + 1) % 8) for dev in range(8)])  56.2 us
  transfers between devices with their start and end apart: 15, of which 15 were waited for; matrix products, arithmetic and copies ran while one was open for 0% of the time, Pallas kernels for 0%

profile of v2, /device:TPU:1, one launch (start us, length us, event | category | flops | bytes accessed | tf_op | source)
XLA Modules:
  0.0 795.8 jit_solution(346837555472726104)
XLA Ops:
  7.2 0.0 copy-start
  7.2 0.0 all-reduce.5.cloned.1.call-start
  7.2 2.6 collective-permute-start
  9.8 5.2 collective-permute-done
  15.0 0.0 collective-permute-start.1
  15.0 4.4 collective-permute-done.1
  19.4 0.0 collective-permute-start.2
  19.4 4.4 collective-permute-done.2
  23.8 4.4 collective-permute-done.3
  28.1 0.7 fusion.23
  28.8 3.7 collective-permute-done.4
  33.2 3.7 collective-permute-done.5
  36.9 0.0 collective-permute-start.6
  36.9 1.3 dynamic-slice
  38.2 3.0 collective-permute-done.6
  41.3 0.7 constant_dynamic-update-slice_fusion
  42.1 0.1 copy_bitcast_fusion
  42.1 2.0 gather_fusion
  44.1 5.3 fusion.4
  49.5 5.1 copy.18
  54.5 5.1 fusion.17
  59.6 248.9 %all-reduce.6 = bf16[64,8192]{1,0:T(8,128)(2,1)} all-reduce(f32[64,8192]{1,0:T(8,128)} %fusion.17), channel_id=2, replica_groups=mesh['col'=64,'row'=8] {'col'}, use_global_device_ids=true, to_apply=%region_0.2.clone | all-reduce | flops 524288 | bytes 3145728
  308.5 1.6 fusion.13
  310.1 0.1 convert_element_type.27
  310.2 53.6 %collective-permute-start.7 = (bf16[128,64]{1,0:T(8,128)(2,1)S(1)}, bf16[128,64]{1,0:T(8,128)(2,1)S(1)}, u32[]{:S(2)}, u32[]{:S(2)}) collective-permute-start(bf16[128,64]{1,0:T(8,128)(2,1)S(1)} %convert_element_type.27), channel_id=1, source_target_pairs={{0,1},{1,2},{2,3},{3,4},{4,5},{5,6},{6,7},{7,0},{8,9},{9,10},{10,1... | collective-permute-start | bytes 49160 | tf_op jit(solution)/shard_map/ppermute | solution.py:24
  363.8 4.7 collective-permute-done.7
  368.6 4.5 collective-permute-done.8
  373.1 4.5 collective-permute-done.9
  377.7 4.5 collective-permute-done.10
  382.2 4.5 collective-permute-done.11
  386.8 4.5 collective-permute-done.12
  391.3 4.5 collective-permute-done.13
  396.0 0.9 fusion.10
  396.9 0.1 copy.20
  397.1 2.0 gather_fusion.1
  399.0 5.3 fusion.7
  404.4 5.1 copy.21
  409.4 5.1 fusion.15
  414.5 0.0 all-reduce.5.cloned.1.call-update
  414.5 259.6 %all-reduce.5.cloned.1.call-done = f32[64,8192]{1,0:T(8,128)} async-done(((f32[64,8192]{1,0:T(8,128)}), f32[64,8192]{1,0:T(8,128)}) %all-reduce.5.cloned.1.call-update) | async-done | bytes 2097168
  674.1 1.7 convert_reduce_fusion
  675.8 0.1 convert_element_type.29
  675.9 0.7 copy.22
  676.6 1.7 dynamic-slice_reduce_fusion
  678.3 0.1 squeeze_reshape.3
  678.4 0.2 fusion.24
  678.6 109.7 %psum.7 = f32[64,64]{1,0:T(8,128)S(1)} all-reduce(f32[64,64]{1,0:T(8,128)S(1)} %fusion.24), channel_id=1, replica_groups=mesh['col'=64,'row'=8] {'col','row'}, use_global_device_ids=true, to_apply=%region_2.4 | all-reduce | flops 4096 | bytes 32768 | tf_op jit(solution)/shard_map/psum | solution.py:40
  788.3 0.6 broadcast_multiply_fusion
  (33 shorter events, 0.2 us)
Async XLA Ops:
  7.2 37.0 %copy-start = (bf16[1,1,96,128,128]{4,3,2,1,0:T(8,128)(2,1)S(1)}, bf16[1,1,96,128,128]{4,3,2,1,0:T(8,128)(2,1)}, u32[]{:S(2)}) copy-start(bf16[1,1,96,128,128]{4,3,2,1,0:T(8,128)(2,1)} %param.8) | copy-start | bytes 9437188
  7.2 667.0 %all-reduce.5.cloned.1.call-start = ((), (), s32[]{:S(2)}) async-start(), calls=%async_computation | async-start | bytes 4194304
  7.2 7.8 collective-permute-start
  15.0 4.4 collective-permute-start.1
  19.4 4.4 collective-permute-start.2
  23.8 4.4 collective-permute-start.3
  28.1 4.4 collective-permute-start.4
  32.5 4.4 collective-permute-start.5
  36.9 4.4 collective-permute-start.6
  49.5 5.1 copy-start.3
  310.2 86.7 %copy-start.1 = (bf16[128,64]{1,0:T(8,128)(2,1)}, bf16[128,64]{1,0:T(8,128)(2,1)S(1)}, u32[]{:S(2)}) copy-start(bf16[128,64]{1,0:T(8,128)(2,1)S(1)} %convert_element_type.27) | copy-start | bytes 49156
  310.2 58.3 %collective-permute-start.7 = (bf16[128,64]{1,0:T(8,128)(2,1)S(1)}, bf16[128,64]{1,0:T(8,128)(2,1)S(1)}, u32[]{:S(2)}, u32[]{:S(2)}) collective-permute-start(bf16[128,64]{1,0:T(8,128)(2,1)S(1)} %convert_element_type.27), channel_id=1, source_target_pairs={{0,1},{1,2},{2,3},{3,4},{4,5},{5,6},{6,7},{7,0},{8,9},{9,10},{10,1... | collective-permute-start | bytes 49160 | tf_op jit(solution)/shard_map/ppermute | solution.py:24
  368.6 4.5 collective-permute-start.8
  373.1 4.6 collective-permute-start.9
  377.7 4.6 collective-permute-start.10
  382.2 4.5 collective-permute-start.11
  386.8 4.6 collective-permute-start.12
  391.3 4.5 collective-permute-start.13
  409.4 269.0 %copy-start.2 = (bf16[128,64]{1,0:T(8,128)(2,1)S(1)}, bf16[128,64]{1,0:T(8,128)(2,1)}, u32[]{:S(2)}) copy-start(bf16[128,64]{1,0:T(8,128)(2,1)} %copy-done.1) | copy-start | bytes 49156
Sparse Core Ops, SparseCore 0:
  414.6 259.4 all-reduce.4

commit v3 on v0

--- a/solution.py
+++ b/solution.py
@@ -30,7 +30,7 @@
     first = apply_local(x_block).astype(jnp.bfloat16)
     second = apply_local(first)
     gram_term = jnp.dot(first[0].astype(jnp.float32).T, second[0], precision=lax.Precision.HIGHEST)
-    gram = lax.psum(gram_term, ("col", "row")) / (n_col * n_row * 128)
+    gram = lax.psum(lax.psum(gram_term, "row"), "col") / (n_col * n_row * 128)
     return (second.astype(jnp.bfloat16), gram)
 
 

time: 761 us -> 957 us (1.26)
  the two profiles are of different devices: /device:TPU:1 before, /device:TPU:2 now
where the time goes in v3:
time: 957 us
  blocking collectives  630 us (66%)
  waiting for transfers between devices  267 us (28%)
  local copies, waits for them, and re-layouts  21.7 us (2%)
  matrix products  21.1 us (2%)
  between operations  14.9 us (2%)
    unnamed x1, blocking collectives  305 us
    psum x2, blocking collectives, local(): gram = lax.psum(lax.psum(gram_term, 'row'), 'col') / (n_col * n_row * 128)  297 us
    unnamed x2, waiting for transfers between devices  267 us
    all_gather x2, blocking collectives, apply_local(): slab_vecs = lax.all_gather(segment[0], 'row', axis=0, tiled=True)  27.4 us
  transfers between devices with their start and end apart: 1, of which 1 were waited for; matrix products, arithmetic and copies ran while one was open for 0% of the time, Pallas kernels for 0%

profile of v3, /device:TPU:2, one launch (start us, length us, event | category | flops | bytes accessed | tf_op | source)
XLA Modules:
  0.0 956.6 jit_solution(5934625358005373638)
XLA Ops:
  7.2 0.0 copy-start
  7.2 0.0 all-reduce.5.cloned.1.call-start
  8.0 0.7 fusion.20
  8.8 15.1 %all-gather = bf16[1,1024,64]{1,2,0:T(8,128)(2,1)S(1)} all-gather(bf16[1,128,64]{1,2,0:T(8,128)(2,1)} %param.5), channel_id=2, replica_groups=mesh['col'=64,'row'=8] {'row'}, dimensions={1}, use_global_device_ids=true | all-gather | bytes 147456 | tf_op jit(solution)/shard_map/all_gather | solution.py:22
  24.0 2.0 gather_fusion
  25.9 0.0 copy-done
  25.9 5.3 fusion.4
  31.3 0.0 copy-start.3
  31.3 5.1 copy.18
  36.3 0.0 copy-done.3
  36.3 5.1 fusion.14
  41.4 305.4 %all-reduce.6 = bf16[64,8192]{1,0:T(8,128)(2,1)} all-reduce(f32[64,8192]{1,0:T(8,128)} %fusion.14), channel_id=3, replica_groups=mesh['col'=64,'row'=8] {'col'}, use_global_device_ids=true, to_apply=%region_0.0.clone | all-reduce | flops 524288 | bytes 3145728
  346.9 1.3 dynamic-slice
  348.2 1.7 fusion.10
  349.9 0.1 convert_element_type.27
  350.0 0.0 copy-start.1
  350.0 12.2 %all_gather.7 = bf16[1024,64]{1,0:T(8,128)(2,1)S(1)} all-gather(bf16[128,64]{1,0:T(8,128)(2,1)S(1)} %convert_element_type.27), channel_id=1, replica_groups=mesh['col'=64,'row'=8] {'row'}, dimensions={0}, use_global_device_ids=true | all-gather | bytes 147456 | tf_op jit(solution)/shard_map/all_gather | solution.py:22
  362.2 0.0 copy-done.1
  362.2 0.1 copy.20
  362.4 2.0 gather_fusion.1
  364.3 5.3 fusion.7
  369.7 5.1 copy.21
  374.7 0.0 copy-start.2
  374.7 5.1 fusion.12
  379.8 0.0 all-reduce.5.cloned.1.call-update
  379.8 267.4 %all-reduce.5.cloned.1.call-done = f32[64,8192]{1,0:T(8,128)} async-done(((f32[64,8192]{1,0:T(8,128)}), f32[64,8192]{1,0:T(8,128)}) %all-reduce.5.cloned.1.call-update) | async-done | bytes 2097168
  647.3 1.7 convert_reduce_fusion
  649.0 0.1 convert_element_type.29
  649.1 0.7 copy.22
  649.8 1.7 dynamic-slice_reduce_fusion
  651.5 0.1 squeeze_reshape.3
  651.6 0.0 copy-done.2
  651.6 0.2 fusion.21
  651.8 20.7 %psum.14 = f32[64,64]{1,0:T(8,128)S(1)} all-reduce(f32[64,64]{1,0:T(8,128)S(1)} %fusion.21), channel_id=1, replica_groups=mesh['col'=64,'row'=8] {'row'}, use_global_device_ids=true, to_apply=%region_2.0 | all-reduce | flops 4096 | bytes 32768 | tf_op jit(solution)/shard_map/psum | solution.py:33
  672.5 276.7 %psum.15 = f32[64,64]{1,0:T(8,128)S(1)} all-reduce(f32[64,64]{1,0:T(8,128)S(1)} %psum.14), channel_id=1, replica_groups=mesh['col'=64,'row'=8] {'col'}, use_global_device_ids=true, to_apply=%region_3.0 | all-reduce | flops 4096 | bytes 32768 | tf_op jit(solution)/shard_map/psum | solution.py:33
  949.2 0.6 broadcast_multiply_fusion
  (4 shorter events, 0.1 us)
Async XLA Ops:
  7.2 18.8 %copy-start = (bf16[1,1,96,128,128]{4,3,2,1,0:T(8,128)(2,1)S(1)}, bf16[1,1,96,128,128]{4,3,2,1,0:T(8,128)(2,1)}, u32[]{:S(2)}) copy-start(bf16[1,1,96,128,128]{4,3,2,1,0:T(8,128)(2,1)} %param.6) | copy-start | bytes 9437188
  7.2 640.1 %all-reduce.5.cloned.1.call-start = ((), (), s32[]{:S(2)}) async-start(), calls=%async_computation | async-start | bytes 4194304
  31.3 5.1 copy-start.3
  350.0 12.2 %copy-start.1 = (bf16[128,64]{1,0:T(8,128)(2,1)}, bf16[128,64]{1,0:T(8,128)(2,1)S(1)}, u32[]{:S(2)}) copy-start(bf16[128,64]{1,0:T(8,128)(2,1)S(1)} %convert_element_type.27) | copy-start | bytes 49156
  374.7 276.9 %copy-start.2 = (bf16[128,64]{1,0:T(8,128)(2,1)S(1)}, bf16[128,64]{1,0:T(8,128)(2,1)}, u32[]{:S(2)}) copy-start(bf16[128,64]{1,0:T(8,128)(2,1)} %copy-done.1) | copy-start | bytes 49156
Sparse Core Ops, SparseCore 0:
  380.0 267.2 all-reduce.4
